TPU v7x, 32 devices: a whole 2x2x4 slice. The times are simulated.
32 devices in a mesh: seq: 8 (over z, y), tp: 4 (over x, core).
Axes of the slice: x: 2, y: 2, z: 4, core: 2. Of those that a mesh axis runs over, the one named last changes fastest.
Arguments:
- tokens: bfloat16 [16384, 1024], P(('seq', 'tp')), may hold values from -6 to 6
- query_weight: bfloat16 [1024, 1024], replicated, may hold values from -0.1875 to 0.1875
- key_weight: bfloat16 [1024, 1024], replicated, may hold values from -0.1875 to 0.1875
- value_weight: bfloat16 [1024, 1024], replicated, may hold values from -0.1875 to 0.1875
- modulate_weight: bfloat16 [1024, 1024], replicated, may hold values from -0.1875 to 0.1875
- output_weight: bfloat16 [1024, 1024], replicated, may hold values from -0.1875 to 0.1875
- gate_weight: bfloat16 [1024, 2816], P(None, 'tp'), may hold values from -0.1875 to 0.1875
- linear_weight: bfloat16 [1024, 2816], P(None, 'tp'), may hold values from -0.1875 to 0.1875
- down_weight: bfloat16 [2816, 1024], P('tp'), may hold values from -0.109375 to 0.109375
- cotangent: bfloat16 [16384, 1024], P(('seq', 'tp')), may hold values from -6 to 6
- decay_exponent: int32 [8], replicated, may hold values from 5 to 17
Outputs:
- mixed: bfloat16 [16384, 1024], P(('seq', 'tp'))
- tokens_grad: float32 [16384, 1024], P(('seq', 'tp'))
- query_grad: float32 [1024, 1024], replicated
- key_grad: float32 [1024, 1024], replicated
- value_grad: float32 [1024, 1024], replicated
- modulate_grad: float32 [1024, 1024], replicated
- output_grad: float32 [1024, 1024], replicated
- gate_grad: float32 [1024, 2816], P('seq', 'tp')
- linear_grad: float32 [1024, 2816], P('seq', 'tp')
- down_grad: float32 [2816, 1024], P('tp', 'seq')
Inputs may be any that keep to these rules, and one draw needn't show every extreme that they name: `decay_exponent`: head h decays by a factor 2 ** (-2 ** (-decay_exponent_h)) a token.
All inputs are finite; a program needn't handle non-finite values.
Results may differ from a plain program's by a relative error of at most 0.015.
Values may be sent and summed in bfloat16 or wider, within the bound.
No kernel may reach another device: no remote copies, remote signals or barrier semaphores. Data moves between devices by JAX's collectives and lax.ppermute only.
A program may use at most 320 MiB of HBM per device.

v0:
```python
import math
import jax
import jax.numpy as jnp
from jax import lax
from jax.sharding import PartitionSpec as P

BLOCK = 256
SEQ_LEN = 16384
EPS = 1e-06
HIGH = lax.Precision.HIGHEST
FLOAT = jnp.float32
BHALF = jnp.bfloat16


def prefix(part, axis, combine, identity, reverse):
    count = lax.axis_size(axis)
    place = lax.axis_index(axis)
    ahead = count - 1 - place if reverse else place
    gathered = jax.tree.map(lambda a: lax.all_gather(a, axis), part)
    state = jax.tree.map(lambda a, e: jnp.zeros_like(a) + jnp.asarray(e, a.dtype), part, identity)

    def one(lap, state):
        source = count - 1 - lap if reverse else lap
        return combine(
            state, jax.tree.map(lambda a: lax.dynamic_index_in_dim(a, source, 0, False), gathered)
        )

    return lax.fori_loop(0, ahead, one, state)


def srms(values):
    return values * lax.rsqrt(jnp.mean(values * values, axis=-1, keepdims=True) + EPS)


def srms_back(values, gradient):
    scaled = lax.rsqrt(jnp.mean(values * values, axis=-1, keepdims=True) + EPS)
    normed = values * scaled
    return scaled * (gradient - normed * jnp.mean(gradient * normed, axis=-1, keepdims=True))


def swish(values):
    return values * jax.nn.sigmoid(values)


def swish_slope(values):
    sigmoid = jax.nn.sigmoid(values)
    return sigmoid * (1.0 + values * (1.0 - sigmoid))


def angles(position, halves):
    column = jnp.arange(halves, dtype=jnp.int32)
    factor = 1 + jnp.right_shift(jnp.full((halves,), 16384, jnp.int32), column // 4)
    phase = position[:, None] * factor[None, :] % 65536
    turned = phase.astype(jnp.float32) * (2.0 * math.pi / 65536.0)
    return (jnp.cos(turned)[:, None, :], jnp.sin(turned)[:, None, :])


def rotate(values, cosine, sine):
    halves = values.shape[-1] // 2
    first = values[..., :halves]
    second = values[..., halves:]
    return jnp.concatenate(
        [first * cosine - second * sine, first * sine + second * cosine], axis=-1
    )


def unrotate(values, cosine, sine):
    halves = values.shape[-1] // 2
    first = values[..., :halves]
    second = values[..., halves:]
    return jnp.concatenate(
        [first * cosine + second * sine, second * cosine - first * sine], axis=-1
    )


def combine(earlier, latter):
    return (earlier[0] * latter[0], latter[0][:, None, None] * earlier[1] + latter[1])


def matmul(left, right):
    return jnp.dot(left, right, preferred_element_type=FLOAT)


def contract_rows(left, right):
    return lax.dot_general(left, right, (((0,), (0,)), ((), ())), preferred_element_type=FLOAT)


def contract_cols(left, right):
    return lax.dot_general(left, right, (((1,), (1,)), ((), ())), preferred_element_type=FLOAT)


def shards(
    tokens,
    query_weight,
    key_weight,
    value_weight,
    modulate_weight,
    output_weight,
    gate_weight,
    linear_weight,
    down_weight,
    cotangent,
    decay_exponent,
):
    tok_count, width = tokens.shape
    heads = decay_exponent.shape[0]
    head_dim = width // heads
    devices = lax.axis_size("seq") * lax.axis_size("tp")
    seq_length = min(SEQ_LEN, tok_count * devices)
    device_place = lax.axis_index("seq") * lax.axis_size("tp") + lax.axis_index("tp")
    first_token = device_place * tok_count
    position = (first_token + jnp.arange(tok_count, dtype=jnp.int32)) % seq_length
    is_start = first_token % seq_length == 0
    decay_rate = jnp.exp2(-decay_exponent.astype(FLOAT))
    cosine, sine = angles(position, head_dim // 2)
    offsets = jnp.arange(BLOCK, dtype=FLOAT)
    distance = offsets[:, None] - offsets[None, :]
    decay_matrix = jnp.where(
        distance[None] >= 0.0,
        jnp.exp2(-jnp.maximum(distance, 0.0)[None] * decay_rate[:, None, None]),
        0.0,
    )
    query_decay = jnp.exp2(-(offsets + 1.0)[:, None] * decay_rate[None, :])[:, :, None]
    key_decay = jnp.exp2(-(BLOCK - 1.0 - offsets)[:, None] * decay_rate[None, :])[:, :, None]
    block_decay = jnp.exp2(-BLOCK * decay_rate)[:, None, None]
    device_decay = jnp.where(is_start, 0.0, jnp.exp2(-tok_count * decay_rate))
    blocks = tok_count // BLOCK
    inputs = tokens.astype(FLOAT)
    normed = srms(inputs).astype(BHALF)
    pre_query = matmul(normed, query_weight)
    pre_key = matmul(normed, key_weight)
    modulate = matmul(normed, modulate_weight)
    query = rotate(swish(pre_query).reshape(tok_count, heads, head_dim), cosine, sine).astype(BHALF)
    keys = rotate(swish(pre_key).reshape(tok_count, heads, head_dim), cosine, sine).astype(BHALF)
    values = matmul(normed, value_weight).astype(BHALF).reshape(tok_count, heads, head_dim)
    key_states = []
    decayed_queries = []
    decayed_keys = []
    local_state = jnp.zeros((heads, head_dim, head_dim), FLOAT)
    for number in range(blocks):
        window = slice(number * BLOCK, (number + 1) * BLOCK)
        decayed_key = (keys[window].astype(FLOAT) * key_decay).astype(BHALF)
        decayed_query = (query[window].astype(FLOAT) * query_decay).astype(BHALF)
        decayed_keys.append(decayed_key)
        decayed_queries.append(decayed_query)
        contrib = jnp.einsum(
            "jhd,jhe->hde", decayed_key, values[window], preferred_element_type=FLOAT
        )
        key_states.append(contrib)
        local_state = block_decay * local_state + contrib
    identity = (jnp.ones_like(device_decay), jnp.zeros_like(local_state))
    carried = prefix((device_decay, local_state), ("seq", "tp"), combine, identity, False)
    state = jnp.where(is_start, 0.0, carried[1])
    pieces = []
    used_states = []
    for number in range(blocks):
        window = slice(number * BLOCK, (number + 1) * BLOCK)
        block_query = query[window]
        scores = jnp.einsum("ihd,jhd->hij", block_query, keys[window], preferred_element_type=FLOAT)
        probs = (scores * decay_matrix).astype(BHALF)
        intra = jnp.einsum("hij,jhd->ihd", probs, values[window], preferred_element_type=FLOAT)
        state_used = state.astype(BHALF)
        inter = jnp.einsum(
            "ihd,hde->ihe", decayed_queries[number], state_used, preferred_element_type=FLOAT
        )
        used_states.append(state_used)
        state = block_decay * state + key_states[number]
        pieces.append(intra + inter)
    attended = jnp.concatenate(pieces, axis=0).reshape(tok_count, width)
    normed_out = srms(attended)
    gated = (normed_out * modulate).astype(BHALF)
    resid = inputs + matmul(gated, output_weight)
    normed_two = srms(resid).astype(BHALF)
    gathered = lax.all_gather(normed_two, "tp", axis=0, tiled=True)
    gate_pre = matmul(gathered, gate_weight)
    linear_pre = matmul(gathered, linear_weight)
    hidden = (gate_pre * linear_pre).astype(BHALF)
    feed = lax.psum_scatter(
        matmul(hidden, down_weight).astype(jnp.bfloat16), "tp", scatter_dimension=0, tiled=True
    ).astype(jnp.float32)
    mixed = (resid + feed).astype(BHALF)
    cot_rows = lax.all_gather(cotangent, "tp", axis=0, tiled=True)
    down_part = contract_rows(hidden, cot_rows)
    hidden_cot = contract_cols(cot_rows, down_weight)
    gate_back = (hidden_cot * linear_pre).astype(BHALF)
    linear_back = (hidden_cot * gate_pre).astype(BHALF)
    gate_part = contract_rows(gathered, gate_back)
    linear_part = contract_rows(gathered, linear_back)
    normed_cot = lax.psum_scatter(
        contract_cols(gate_back, gate_weight) + contract_cols(linear_back, linear_weight),
        "tp",
        scatter_dimension=0,
        tiled=True,
    )
    gate_grad, linear_grad, down_grad = (
        lax.psum_scatter(
            gate_part.astype(jnp.bfloat16), "seq", scatter_dimension=0, tiled=True
        ).astype(jnp.float32),
        lax.psum_scatter(
            linear_part.astype(jnp.bfloat16), "seq", scatter_dimension=0, tiled=True
        ).astype(jnp.float32),
        lax.psum_scatter(
            down_part.astype(jnp.bfloat16), "seq", scatter_dimension=1, tiled=True
        ).astype(jnp.float32),
    )
    resid_cot = cotangent.astype(FLOAT) + srms_back(resid, normed_cot)
    branch_back = resid_cot.astype(BHALF)
    output_part = contract_rows(gated, branch_back)
    gated_cot = contract_cols(branch_back, output_weight)
    modulate_back = (gated_cot * normed_out).astype(BHALF)
    attended_back = (
        srms_back(attended, gated_cot * modulate).astype(BHALF).reshape(tok_count, heads, head_dim)
    )
    direct = []
    for number in range(blocks):
        window = slice(number * BLOCK, (number + 1) * BLOCK)
        direct.append(
            jnp.einsum(
                "ihd,ihe->hde",
                decayed_queries[number],
                attended_back[window],
                preferred_element_type=FLOAT,
            )
        )
    inbound = jnp.zeros_like(local_state)
    for number in reversed(range(blocks)):
        inbound = block_decay * inbound + direct[number]
    masked = jnp.where(is_start, 0.0, inbound)
    after = prefix((device_decay, masked), ("seq", "tp"), combine, identity, True)
    outer = after[1]
    accum = jnp.zeros_like(local_state)
    query_parts = []
    key_parts = []
    value_parts = []
    for number in reversed(range(blocks)):
        window = slice(number * BLOCK, (number + 1) * BLOCK)
        state_cot = outer + accum
        outer = block_decay * outer
        accum = block_decay * accum + direct[number]
        block_query = query[window]
        block_key = keys[window]
        block_value = values[window]
        block_back = attended_back[window]
        key_part = (
            jnp.einsum("hde,jhe->jhd", state_cot, block_value.astype(FLOAT), precision=HIGH)
            * key_decay
        )
        value_part = jnp.einsum(
            "jhd,hde->jhe", decayed_keys[number].astype(FLOAT), state_cot, precision=HIGH
        )
        scores = jnp.einsum("ihd,jhd->hij", block_query, block_key, preferred_element_type=FLOAT)
        probs = (scores * decay_matrix).astype(BHALF)
        prob_cot = jnp.einsum("ihe,jhe->hij", block_back, block_value, preferred_element_type=FLOAT)
        score_back = (prob_cot * decay_matrix).astype(BHALF)
        value_part = value_part + jnp.einsum(
            "hij,ihe->jhe", probs, block_back, preferred_element_type=FLOAT
        )
        key_part = key_part + jnp.einsum(
            "hij,ihd->jhd", score_back, block_query, preferred_element_type=FLOAT
        )
        query_part = jnp.einsum("hij,jhd->ihd", score_back, block_key, preferred_element_type=FLOAT)
        query_part = (
            query_part
            + jnp.einsum(
                "ihe,hde->ihd", block_back, used_states[number], preferred_element_type=FLOAT
            )
            * query_decay
        )
        query_parts.insert(0, query_part)
        key_parts.insert(0, key_part)
        value_parts.insert(0, value_part)
    query_cot = jnp.concatenate(query_parts, axis=0)
    key_cot = jnp.concatenate(key_parts, axis=0)
    value_cot = jnp.concatenate(value_parts, axis=0)
    query_back = (
        unrotate(query_cot, cosine, sine).reshape(tok_count, width) * swish_slope(pre_query)
    ).astype(BHALF)
    key_back = (
        unrotate(key_cot, cosine, sine).reshape(tok_count, width) * swish_slope(pre_key)
    ).astype(BHALF)
    value_back = value_cot.reshape(tok_count, width).astype(BHALF)
    normed_grad = contract_cols(query_back, query_weight) + contract_cols(key_back, key_weight)
    normed_grad = (
        normed_grad
        + contract_cols(value_back, value_weight)
        + contract_cols(modulate_back, modulate_weight)
    )
    tokens_grad = resid_cot + srms_back(inputs, normed_grad)
    query_grad, key_grad, value_grad, modulate_grad, output_grad = lax.psum(
        (
            contract_rows(normed, query_back),
            contract_rows(normed, key_back),
            contract_rows(normed, value_back),
            contract_rows(normed, modulate_back),
            output_part,
        ),
        ("seq", "tp"),
    )
    return (
        mixed,
        tokens_grad,
        query_grad,
        key_grad,
        value_grad,
        modulate_grad,
        output_grad,
        gate_grad,
        linear_grad,
        down_grad,
    )


def solution(mesh):
    return jax.shard_map(
        shards,
        mesh=mesh,
        in_specs=(
            P(("seq", "tp"), None),
            P(),
            P(),
            P(),
            P(),
            P(),
            P(None, "tp"),
            P(None, "tp"),
            P("tp", None),
            P(("seq", "tp"), None),
            P(),
        ),
        out_specs=(
            P(("seq", "tp"), None),
            P(("seq", "tp"), None),
            P(),
            P(),
            P(),
            P(),
            P(),
            P("seq", "tp"),
            P("seq", "tp"),
            P("tp", "seq"),
        ),
        check_vma=False,
    )
```

profile of v0, /device:TPU:0, one launch (start us, length us, event | category | flops | bytes accessed | tf_op | source)
XLA Modules:
  0.0 1147.0 jit_solution(10695310475397209086)
XLA Ops:
  9.7 3.3 convolution_convert_fusion.4
  19.4 2.7 fusion.80
  22.1 2.7 fusion.79
  26.5 5.1 subtract_convert_fusion
  31.6 2.1 fusion.25
  37.9 42.9 %all-reduce = f32[256]{0:T(256)S(1)} all-reduce(f32[256]{0:T(256)S(1)} %get-tuple-element.206), channel_id=2, replica_groups=mesh['seq'=8,'tp'=4] {'seq','tp'}, use_global_device_ids=true, to_apply=%add | all-reduce | flops 256 | bytes 2048
  87.4 69.5 %all-gather.12.cloned.1.call-done = f32[256,128,128]{2,1,0:T(8,128)} async-done(((f32[8,128,128]{2,1,0:T(8,128)}), f32[256,128,128]{2,1,0:T(8,128)}) %all-gather.12.cloned.1.call-update) | async-done | bytes 16777232 | tf_op jit(solution)/shard_map/all_gather | solution.py:19
  159.0 2.1 fusion.19
  163.6 2.9 copy.115
  166.5 4.8 multiply_convert_fusion.7
  176.1 98.1 %all-gather.8.cloned.1.call-done = bf16[2048,1024]{1,0:T(8,128)(2,1)} async-done(((bf16[512,1024]{1,0:T(8,128)(2,1)}), bf16[2048,1024]{1,0:T(8,128)(2,1)}) %all-gather.8.cloned.1.call-update) | async-done | bytes 4194320 | tf_op jit(solution)/shard_map/all_gather | solution.py:174
  274.3 8.4 fusion.83
  282.7 5.1 fusion.82
  287.8 22.6 %all-gather.10.cloned.1.call-done = bf16[2048,1024]{1,0:T(8,128)(2,1)} async-done(((bf16[512,1024]{1,0:T(8,128)(2,1)}), bf16[2048,1024]{1,0:T(8,128)(2,1)}) %all-gather.10.cloned.1.call-update) | async-done | bytes 4194320 | tf_op jit(solution)/shard_map/all_gather | solution.py:182
  310.3 11.0 multiply_convert_fusion
  321.4 3.5 fusion.84
  324.9 6.0 convolution_add_fusion
  331.2 7.7 convolution_convert_fusion
  339.0 63.8 %reduce-scatter.14.cloned.1.call-done = f32[512,1024]{1,0:T(8,128)} async-done(((f32[2048,1024]{1,0:T(8,128)}), f32[512,1024]{1,0:T(8,128)}) %reduce-scatter.14.cloned.1.call-update) | async-done | bytes 2097168 | tf_op jit(solution)/shard_map/reduce_scatter | solution.py:189
  402.8 2.6 multiply_reduce_fusion.1
  405.4 45.1 %reduce-scatter.12.cloned.1.call-done = bf16[512,1024]{1,0:T(8,128)(2,1)} async-done(((bf16[2048,1024]{1,0:T(8,128)(2,1)}), bf16[512,1024]{1,0:T(8,128)(2,1)}) %reduce-scatter.12.cloned.1.call-update) | async-done | bytes 1048592 | tf_op jit(solution)/shard_map/reduce_scatter | solution.py:178
  450.5 4.5 multiply_add_fusion.2
  455.0 2.6 multiply_reduce_fusion
  462.0 2.8 fusion.24
  464.8 7.3 convolution_convert_fusion.3
  472.1 2.7 copy.166
  475.3 7.3 convolution_convert_fusion.1
  482.6 2.6 copy.164
  485.3 7.3 convolution_convert_fusion.2
  492.6 2.6 copy.162
  502.4 3.3 fusion.38
  508.8 3.4 fusion.64
  512.2 67.6 %all-gather.14.cloned.1.call-done = f32[256,128,128]{2,1,0:T(8,128)} async-done(((f32[8,128,128]{2,1,0:T(8,128)}), f32[256,128,128]{2,1,0:T(8,128)}) %all-gather.14.cloned.1.call-update) | async-done | bytes 16777232 | tf_op jit(solution)/shard_map/all_gather | solution.py:19
  579.8 38.5 %while.27 = (s32[]{:T(128)}, f32[8,128,128]{2,1,0:T(8,128)S(1)}, s32[]{:T(128)}, f32[32,8]{1,0:T(8,128)S(1)}, f32[32,8,128,128]{3,2,1,0:T(8,128)}, /*index=5*/s32[]{:T(128)}, s32[]{:T(128)}, s32[]{:T(128)}, s32[]{:T(128)}) while((s32[]{:T(128)}, f32[8,128,128]{2,1,0:T(8,128)S(1)}, s32[]{:T(128)}, f32[32,8]{1,0:T(8,128)S(1)}, ...), condition=%wide.region_10.11_spmd, body=%wide.region_9.10_spmd.sunk | while | flops 262150 | bytes 1573115 | solution.py:28
  618.4 2.2 fusion.42
  627.2 3.5 fusion.66
  633.3 3.4 fusion.70
  638.6 3.4 fusion.68
  642.0 4.3 reduce-scatter.20.cloned.1.call-done
  648.2 65.8 %reduce-scatter.18.cloned.1.call-done = bf16[128,704]{1,0:T(8,128)(2,1)} async-done(((bf16[1024,704]{1,0:T(8,128)(2,1)}), bf16[128,704]{1,0:T(8,128)(2,1)}) %reduce-scatter.18.cloned.1.call-update) | async-done | bytes 180240
  715.8 66.0 %reduce-scatter.16.cloned.1.call-done = bf16[128,704]{1,0:T(8,128)(2,1)} async-done(((bf16[1024,704]{1,0:T(8,128)(2,1)}), bf16[128,704]{1,0:T(8,128)(2,1)}) %reduce-scatter.16.cloned.1.call-update) | async-done | bytes 180240
  783.7 3.0 fusion.87
  794.0 326.8 %all-reduce.4.cloned.1.call-done = (f32[1024,1024]{1,0:T(8,128)}, f32[1024,1024]{1,0:T(8,128)}, f32[1024,1024]{1,0:T(8,128)}, f32[1024,1024]{1,0:T(8,128)}, f32[1024,1024]{1,0:T(8,128)}) async-done(((f32[1024,1024]{1,0:T(8,128)}, f32[1024,1024]{1,0:T(8,128)}, f32[1024,1024]{1,0:T(8,128)}, f32[1024,1024]{1,0:T(8,128)}, f32[1024,1024]{1,0:T(8,128)}), (f32[1024,1024]{1,0:T(8,128)}, f32[1024,1024]{1,0:T(8,128)}, ...) | async-done | bytes 20971536 | tf_op jit(solution)/shard_map/psum | solution.py:289
  1120.8 4.9 copy.240
  1125.8 2.1 copy.241
  1129.5 2.1 copy.242
  1133.2 2.1 copy.243
  1136.9 2.1 copy.244
  (317 shorter events, 112.6 us)
Async XLA Ops:
  7.2 164.2 %copy-start = (bf16[1024,1024]{1,0:T(8,128)(2,1)S(1)}, bf16[1024,1024]{1,0:T(8,128)(2,1)}, u32[]{:S(2)}) copy-start(bf16[1024,1024]{1,0:T(8,128)(2,1)} %param.20) | copy-start | bytes 6291460
  7.2 149.7 %all-gather.12.cloned.1.call-start = ((), (), s32[]{:S(2)}) async-start(), calls=%async_computation.9 | async-start | bytes 17301504 | tf_op jit(solution)/shard_map/all_gather | solution.py:19
  9.6 4.4 copy-start.2
  9.6 4.4 copy-start.77
  25.8 5.8 copy-start.66
  31.6 2.9 copy-start.27
  31.6 4.6 copy-start.36
  37.8 236.5 %all-gather.8.cloned.1.call-start = ((), (), s32[]{:S(2)}) async-start(), calls=%async_computation.5 | async-start | bytes 5242880 | tf_op jit(solution)/shard_map/all_gather | solution.py:174
  157.7 3.4 copy-start.24
  157.7 3.4 copy-start.65
  175.2 135.2 %all-gather.10.cloned.1.call-start = ((), (), s32[]{:S(2)}) async-start(), calls=%async_computation.7 | async-start | bytes 5242880 | tf_op jit(solution)/shard_map/all_gather | solution.py:182
  175.9 226.9 %reduce-scatter.14.cloned.1.call-start = ((), (), s32[]{:S(2)}) async-start(), calls=%async_computation.8 | async-start | bytes 10485760 | tf_op jit(solution)/shard_map/reduce_scatter | solution.py:189
  274.3 8.4 copy-start.74
  274.3 8.4 copy-start.79
  310.3 11.0 copy-start.80
  321.4 3.5 copy-start.14
  321.4 3.5 copy-start.15
  321.4 3.5 copy-start.81
  330.9 119.5 %reduce-scatter.12.cloned.1.call-start = ((), (), s32[]{:S(2)}) async-start(), calls=%async_computation.6 | async-start | bytes 5242880 | tf_op jit(solution)/shard_map/reduce_scatter | solution.py:178
  339.0 240.8 %all-gather.14.cloned.1.call-start = ((), (), s32[]{:S(2)}) async-start(), calls=%async_computation.10 | async-start | bytes 17301504 | tf_op jit(solution)/shard_map/all_gather | solution.py:19
  450.5 4.5 copy-start.3
  450.5 4.5 copy-start.9
  458.8 3.1 copy-start.35
  459.1 39.9 %copy-start.40 = (bf16[256,1024]{0,1:T(8,128)(2,1)}, bf16[256,1024]{0,1:T(8,128)(2,1)S(1)}, u32[]{:S(2)}) copy-start(bf16[256,1024]{0,1:T(8,128)(2,1)S(1)} %copy.173) | copy-start | bytes 1572868
  462.0 33.3 %copy-start.44 = (bf16[256,1024]{0,1:T(8,128)(2,1)}, bf16[256,1024]{0,1:T(8,128)(2,1)S(1)}, u32[]{:S(2)}) copy-start(bf16[256,1024]{0,1:T(8,128)(2,1)S(1)} %copy.172) | copy-start | bytes 1572868
  464.8 181.6 %reduce-scatter.20.cloned.1.call-start = ((), (), s32[]{:S(2)}) async-start(), calls=%async_computation.13 | async-start | bytes 1769472
  474.8 239.2 %reduce-scatter.18.cloned.1.call-start = ((), (), s32[]{:S(2)}) async-start(), calls=%async_computation.12 | async-start | bytes 1769472
  485.3 296.6 %reduce-scatter.16.cloned.1.call-start = ((), (), s32[]{:S(2)}) async-start(), calls=%async_computation.11 | async-start | bytes 1769472
  495.3 625.5 %all-reduce.4.cloned.1.call-start = ((), (), s32[]{:S(2)}) async-start(), calls=%async_computation.14 | async-start | bytes 41943040 | tf_op jit(solution)/shard_map/psum | solution.py:289
  502.4 3.3 copy-start.4
  502.4 3.3 copy-start.45
  579.8 38.5 %copy-start.22 = (bf16[256,8,128]{2,0,1:T(8,128)(2,1)S(1)}, bf16[256,8,128]{2,0,1:T(8,128)(2,1)}, u32[]{:S(2)}) copy-start(bf16[256,8,128]{2,0,1:T(8,128)(2,1)} %copy-done.20) | copy-start | bytes 1572868
  618.4 3.2 copy-start.30
  618.4 3.2 copy-start.47
  618.4 3.2 copy-start.64
  627.2 3.5 copy-start.57
  627.2 3.5 copy-start.63
  627.2 3.5 copy-start.67
  633.2 3.4 copy-start.49
  633.2 3.4 copy-start.17
  642.0 141.7 %copy-start.71 = (bf16[512,8,128]{0,2,1:T(8,128)(2,1)S(1)}, bf16[512,8,128]{0,2,1:T(8,128)(2,1)}, u32[]{:S(2)}) copy-start(bf16[512,8,128]{0,2,1:T(8,128)(2,1)} %copy-done.70) | copy-start | bytes 3145732
  783.7 3.0 copy-start.52
  783.7 3.1 copy-start.76
  1120.8 4.9 copy-start.62
  1125.8 3.7 copy-start.61
  1129.5 3.7 copy-start.60
  1133.2 3.7 copy-start.59
  1136.9 3.1 copy-start.1
  (44 other events, 72.7 us)
Sparse Core Ops, SparseCore 0:
  37.9 118.8 all-gather.11
  175.3 98.9 all-gather.7
  275.8 34.4 all-gather.9
  331.1 71.7 reduce-scatter.13
  405.9 44.5 reduce-scatter.11
  464.9 114.8 all-gather.13
  583.2 63.0 reduce-scatter.19
  650.1 63.7 reduce-scatter.17
  718.0 63.8 reduce-scatter.15
  789.8 330.9 all-reduce.3
where the time goes:
time: 1160 us; the launch traced here: 1150 us
  waiting for transfers between devices  831 us (72%)
  matrix products  132 us (11%)
  other arithmetic  68.9 us (6%)
  local copies, waits for them, and re-layouts  54.8 us (5%)
  blocking collectives  42.9 us (4%)
  between operations  15.3 us (1%)
    psum x1, waiting for transfers between devices, shards(): lax.psum((contract_rows(normed, query_back), contract_rows(normed, key_ba...  327 us
    all_gather x2, waiting for transfers between devices, prefix(): gathered = jax.tree.map(lambda a: lax.all_gather(a, axis), part)  137 us
    unnamed x13, waiting for transfers between devices  137 us
    all_gather x1, waiting for transfers between devices, shards(): gathered = lax.all_gather(normed_two, 'tp', axis=0, tiled=True)  98.1 us
    reduce_scatter x1, waiting for transfers between devices, shards(): lax.psum_scatter(contract_cols(gate_back, gate_weight) + contract_cols(li...  63.8 us
    reduce_scatter x1, waiting for transfers between devices, shards(): lax.psum_scatter(matmul(hidden, down_weight).astype(jnp.bfloat16), 'tp',...  45.1 us
    unnamed x179, local copies, waits for them, and re-layouts  43 us
    unnamed x1, blocking collectives  42.9 us
  transfers between devices with their start and end apart: 10, of which 10 were waited for; matrix products, arithmetic and copies ran while one was open for 13% of the time, Pallas kernels for 0%

commit v1 on v0

--- a/solution.py
+++ b/solution.py
@@ -287,14 +287,17 @@
     )
     tokens_grad = resid_cot + srms_back(inputs, normed_grad)
     query_grad, key_grad, value_grad, modulate_grad, output_grad = lax.psum(
-        (
-            contract_rows(normed, query_back),
-            contract_rows(normed, key_back),
-            contract_rows(normed, value_back),
-            contract_rows(normed, modulate_back),
-            output_part,
+        lax.psum(
+            (
+                contract_rows(normed, query_back),
+                contract_rows(normed, key_back),
+                contract_rows(normed, value_back),
+                contract_rows(normed, modulate_back),
+                output_part,
+            ),
+            "tp",
         ),
-        ("seq", "tp"),
+        "seq",
     )
     return (
         mixed,

time: 1160 us -> 1870 us (1.61)
  waiting for transfers between devices: 831 us -> 1550 us
    psum x0 -> x1, waiting for transfers between devices: none -> 622 us  [shards(): lax.psum(lax.psum((contract_rows(normed, query_back), contract_rows(norme...]
    unnamed x13 -> x14, waiting for transfers between devices: 137 us -> 201 us
    all_gather x2, waiting for transfers between devices: 137 us -> 168 us  [prefix(): gathered = jax.tree.map(lambda a: lax.all_gather(a, axis), part)]
    unnamed x179 -> x177, local copies, waits for them, and re-layouts: 43 us -> 40.5 us
  transfers between devices with their start and end apart: 10 -> 11, of which waited for: 10 -> 11; matrix products, arithmetic and copies ran while one was open for 13% -> 5% of each run, Pallas kernels for 0% -> 0%
where the time goes in v1:
time: 1870 us; the launch traced here: 1860 us
  waiting for transfers between devices  1550 us (83%)
  matrix products  130 us (7%)
  other arithmetic  68.8 us (4%)
  local copies, waits for them, and re-layouts  53.6 us (3%)
  blocking collectives  42.9 us (2%)
    psum x1, waiting for transfers between devices, shards(): lax.psum(lax.psum((contract_rows(normed, query_back), contract_rows(norme...  622 us
    psum x1, waiting for transfers between devices, shards(): lax.psum((contract_rows(normed, query_back), contract_rows(normed, key_ba...  329 us
    unnamed x14, waiting for transfers between devices  201 us
    all_gather x2, waiting for transfers between devices, prefix(): gathered = jax.tree.map(lambda a: lax.all_gather(a, axis), part)  168 us
    all_gather x1, waiting for transfers between devices, shards(): gathered = lax.all_gather(normed_two, 'tp', axis=0, tiled=True)  97.8 us
    reduce_scatter x1, waiting for transfers between devices, shards(): lax.psum_scatter(contract_cols(gate_back, gate_weight) + contract_cols(li...  63.6 us
    reduce_scatter x1, waiting for transfers between devices, shards(): lax.psum_scatter(matmul(hidden, down_weight).astype(jnp.bfloat16), 'tp',...  45.1 us
    unnamed x1, blocking collectives  42.9 us
  transfers between devices with their start and end apart: 11, of which 11 were waited for; matrix products, arithmetic and copies ran while one was open for 5% of the time, Pallas kernels for 0%

profile of v1, /device:TPU:0, one launch (start us, length us, event | category | flops | bytes accessed | tf_op | source)
XLA Modules:
  0.0 1863.1 jit_solution(17924168015565770929)
XLA Ops:
  9.7 3.3 convolution_convert_fusion.4
  19.4 2.7 fusion.80
  22.0 2.7 fusion.79
  26.4 5.1 subtract_convert_fusion
  31.6 2.1 fusion.25
  37.9 42.9 %all-reduce = f32[256]{0:T(256)S(1)} all-reduce(f32[256]{0:T(256)S(1)} %get-tuple-element.211), channel_id=2, replica_groups=mesh['seq'=8,'tp'=4] {'seq','tp'}, use_global_device_ids=true, to_apply=%add | all-reduce | flops 256 | bytes 2048
  81.0 2.0 multiply_convert_fusion.9
  87.4 69.5 %all-gather.12.cloned.1.call-done = f32[256,128,128]{2,1,0:T(8,128)} async-done(((f32[8,128,128]{2,1,0:T(8,128)}), f32[256,128,128]{2,1,0:T(8,128)}) %all-gather.12.cloned.1.call-update) | async-done | bytes 16777232 | tf_op jit(solution)/shard_map/all_gather | solution.py:19
  159.0 2.1 fusion.19
  163.6 2.9 copy.115
  166.5 4.8 multiply_convert_fusion.7
  176.1 97.8 %all-gather.8.cloned.1.call-done = bf16[2048,1024]{1,0:T(8,128)(2,1)} async-done(((bf16[512,1024]{1,0:T(8,128)(2,1)}), bf16[2048,1024]{1,0:T(8,128)(2,1)}) %all-gather.8.cloned.1.call-update) | async-done | bytes 4194320 | tf_op jit(solution)/shard_map/all_gather | solution.py:174
  274.0 8.4 fusion.83
  282.4 5.0 fusion.82
  287.4 22.7 %all-gather.10.cloned.1.call-done = bf16[2048,1024]{1,0:T(8,128)(2,1)} async-done(((bf16[512,1024]{1,0:T(8,128)(2,1)}), bf16[2048,1024]{1,0:T(8,128)(2,1)}) %all-gather.10.cloned.1.call-update) | async-done | bytes 4194320 | tf_op jit(solution)/shard_map/all_gather | solution.py:182
  310.1 11.0 multiply_convert_fusion
  321.1 3.5 fusion.84
  324.6 6.0 convolution_add_fusion
  331.1 7.7 convolution_convert_fusion
  338.9 63.6 %reduce-scatter.14.cloned.1.call-done = f32[512,1024]{1,0:T(8,128)} async-done(((f32[2048,1024]{1,0:T(8,128)}), f32[512,1024]{1,0:T(8,128)}) %reduce-scatter.14.cloned.1.call-update) | async-done | bytes 2097168 | tf_op jit(solution)/shard_map/reduce_scatter | solution.py:189
  402.5 2.6 multiply_reduce_fusion.1
  405.1 45.1 %reduce-scatter.12.cloned.1.call-done = bf16[512,1024]{1,0:T(8,128)(2,1)} async-done(((bf16[2048,1024]{1,0:T(8,128)(2,1)}), bf16[512,1024]{1,0:T(8,128)(2,1)}) %reduce-scatter.12.cloned.1.call-update) | async-done | bytes 1048592 | tf_op jit(solution)/shard_map/reduce_scatter | solution.py:178
  450.2 4.5 multiply_add_fusion.2
  454.7 2.5 multiply_reduce_fusion
  463.7 2.8 fusion.24
  466.6 2.0 multiply_convert_fusion.5
  476.2 3.4 fusion.64
  479.7 3.3 fusion.38
  483.0 98.5 %all-gather.14.cloned.1.call-done = f32[256,128,128]{2,1,0:T(8,128)} async-done(((f32[8,128,128]{2,1,0:T(8,128)}), f32[256,128,128]{2,1,0:T(8,128)}) %all-gather.14.cloned.1.call-update) | async-done | bytes 16777232 | tf_op jit(solution)/shard_map/all_gather | solution.py:19
  581.6 38.4 %while.27 = (s32[]{:T(128)}, f32[8,128,128]{2,1,0:T(8,128)S(1)}, s32[]{:T(128)}, f32[32,8]{1,0:T(8,128)S(1)}, f32[32,8,128,128]{3,2,1,0:T(8,128)}, /*index=5*/s32[]{:T(128)}, s32[]{:T(128)}, s32[]{:T(128)}, s32[]{:T(128)}) while((s32[]{:T(128)}, f32[8,128,128]{2,1,0:T(8,128)S(1)}, s32[]{:T(128)}, f32[32,8]{1,0:T(8,128)S(1)}, ...), condition=%wide.region_10.11_spmd, body=%wide.region_9.10_spmd.sunk | while | flops 262150 | bytes 1573115 | solution.py:28
  620.0 2.2 fusion.42
  628.8 3.5 fusion.66
  634.9 3.4 fusion.70
  640.2 3.4 fusion.68
  643.9 7.5 convolution_convert_fusion.3
  653.0 6.3 convolution_convert_fusion.1
  661.0 6.3 convolution_convert_fusion.2
  669.2 328.9 %all-reduce.8.cloned.1.call-done = (f32[1024,1024]{1,0:T(8,128)}, f32[1024,1024]{1,0:T(8,128)}, f32[1024,1024]{1,0:T(8,128)}, f32[1024,1024]{1,0:T(8,128)}, f32[1024,1024]{1,0:T(8,128)}) async-done(((f32[1024,1024]{1,0:T(8,128)}, f32[1024,1024]{1,0:T(8,128)}, f32[1024,1024]{1,0:T(8,128)}, f32[1024,1024]{1,0:T(8,128)}, f32[1024,1024]{1,0:T(8,128)}), (f32[1024,1024]{1,0:T(8,128)}, f32[1024,1024]{1,0:T(8,128)}, ...) | async-done | bytes 20971536 | tf_op jit(solution)/shard_map/psum | solution.py:290
  998.1 68.7 %reduce-scatter.20.cloned.1.call-done = bf16[128,704]{1,0:T(8,128)(2,1)} async-done(((bf16[1024,704]{1,0:T(8,128)(2,1)}), bf16[128,704]{1,0:T(8,128)(2,1)}) %reduce-scatter.20.cloned.1.call-update) | async-done | bytes 180240
  1068.6 65.3 %reduce-scatter.18.cloned.1.call-done = bf16[128,704]{1,0:T(8,128)(2,1)} async-done(((bf16[1024,704]{1,0:T(8,128)(2,1)}), bf16[128,704]{1,0:T(8,128)(2,1)}) %reduce-scatter.18.cloned.1.call-update) | async-done | bytes 180240
  1135.8 66.3 %reduce-scatter.16.cloned.1.call-done = bf16[128,704]{1,0:T(8,128)(2,1)} async-done(((bf16[1024,704]{1,0:T(8,128)(2,1)}), bf16[128,704]{1,0:T(8,128)(2,1)}) %reduce-scatter.16.cloned.1.call-update) | async-done | bytes 180240
  1203.9 3.0 fusion.87
  1214.9 622.2 %all-reduce.6.cloned.1.call-done = (f32[1024,1024]{1,0:T(8,128)}, f32[1024,1024]{1,0:T(8,128)}, f32[1024,1024]{1,0:T(8,128)}, f32[1024,1024]{1,0:T(8,128)}, f32[1024,1024]{1,0:T(8,128)}) async-done(((f32[1024,1024]{1,0:T(8,128)}, f32[1024,1024]{1,0:T(8,128)}, f32[1024,1024]{1,0:T(8,128)}, f32[1024,1024]{1,0:T(8,128)}, f32[1024,1024]{1,0:T(8,128)}), (f32[1024,1024]{1,0:T(8,128)}, f32[1024,1024]{1,0:T(8,128)}, ...) | async-done | bytes 20971536 | tf_op jit(solution)/shard_map/psum | solution.py:289
  1837.1 4.9 copy.245
  1842.0 2.1 copy.246
  1845.8 2.1 copy.247
  1849.5 2.1 copy.248
  1853.2 2.1 copy.249
  (318 shorter events, 115.8 us)
Async XLA Ops:
  7.2 164.1 %copy-start = (bf16[1024,1024]{1,0:T(8,128)(2,1)S(1)}, bf16[1024,1024]{1,0:T(8,128)(2,1)}, u32[]{:S(2)}) copy-start(bf16[1024,1024]{1,0:T(8,128)(2,1)} %param.20) | copy-start | bytes 6291460
  7.2 149.7 %all-gather.12.cloned.1.call-start = ((), (), s32[]{:S(2)}) async-start(), calls=%async_computation.9 | async-start | bytes 17301504 | tf_op jit(solution)/shard_map/all_gather | solution.py:19
  9.6 4.4 copy-start.2
  9.6 4.4 copy-start.76
  25.8 5.8 copy-start.65
  31.6 4.7 copy-start.35
  37.8 236.2 %all-gather.8.cloned.1.call-start = ((), (), s32[]{:S(2)}) async-start(), calls=%async_computation.5 | async-start | bytes 5242880 | tf_op jit(solution)/shard_map/all_gather | solution.py:174
  157.7 3.4 copy-start.24
  157.7 3.4 copy-start.64
  175.2 134.9 %all-gather.10.cloned.1.call-start = ((), (), s32[]{:S(2)}) async-start(), calls=%async_computation.7 | async-start | bytes 5242880 | tf_op jit(solution)/shard_map/all_gather | solution.py:182
  175.9 226.6 %reduce-scatter.14.cloned.1.call-start = ((), (), s32[]{:S(2)}) async-start(), calls=%async_computation.8 | async-start | bytes 10485760 | tf_op jit(solution)/shard_map/reduce_scatter | solution.py:189
  274.0 8.4 copy-start.73
  274.0 8.4 copy-start.78
  310.1 11.0 copy-start.79
  321.1 3.5 copy-start.14
  321.1 3.5 copy-start.15
  321.1 3.5 copy-start.80
  330.6 119.5 %reduce-scatter.12.cloned.1.call-start = ((), (), s32[]{:S(2)}) async-start(), calls=%async_computation.6 | async-start | bytes 5242880 | tf_op jit(solution)/shard_map/reduce_scatter | solution.py:178
  338.8 242.7 %all-gather.14.cloned.1.call-start = ((), (), s32[]{:S(2)}) async-start(), calls=%async_computation.10 | async-start | bytes 17301504 | tf_op jit(solution)/shard_map/all_gather | solution.py:19
  450.2 4.5 copy-start.3
  450.2 4.5 copy-start.9
  457.7 3.2 copy-start.25
  458.7 5.0 copy-start.34
  462.4 4.2 copy-start.28
  466.5 531.6 %all-reduce.8.cloned.1.call-start = ((), (), s32[]{:S(2)}) async-start(), calls=%async_computation.15 | async-start | bytes 41943040 | tf_op jit(solution)/shard_map/psum | solution.py:290
  476.2 3.4 copy-start.6
  476.2 3.4 copy-start.13
  581.6 38.4 %copy-start.22 = (bf16[256,8,128]{2,0,1:T(8,128)(2,1)S(1)}, bf16[256,8,128]{2,0,1:T(8,128)(2,1)}, u32[]{:S(2)}) copy-start(bf16[256,8,128]{2,0,1:T(8,128)(2,1)} %copy-done.20) | copy-start | bytes 1572868
  620.0 3.2 copy-start.29
  620.0 3.2 copy-start.46
  620.0 3.2 copy-start.63
  628.8 3.5 copy-start.56
  628.8 3.5 copy-start.62
  628.8 3.5 copy-start.66
  634.8 3.4 copy-start.48
  634.8 3.4 copy-start.17
  643.6 423.2 %reduce-scatter.20.cloned.1.call-start = ((), (), s32[]{:S(2)}) async-start(), calls=%async_computation.13 | async-start | bytes 1769472
  653.0 481.0 %reduce-scatter.18.cloned.1.call-start = ((), (), s32[]{:S(2)}) async-start(), calls=%async_computation.12 | async-start | bytes 1769472
  660.9 541.2 %reduce-scatter.16.cloned.1.call-start = ((), (), s32[]{:S(2)}) async-start(), calls=%async_computation.11 | async-start | bytes 1769472
  668.9 1168.2 %all-reduce.6.cloned.1.call-start = ((), (), s32[]{:S(2)}) async-start(), calls=%async_computation.14 | async-start | bytes 41943040 | tf_op jit(solution)/shard_map/psum | solution.py:289
  998.1 205.8 %copy-start.70 = (bf16[512,8,128]{0,2,1:T(8,128)(2,1)S(1)}, bf16[512,8,128]{0,2,1:T(8,128)(2,1)}, u32[]{:S(2)}) copy-start(bf16[512,8,128]{0,2,1:T(8,128)(2,1)} %copy-done.69) | copy-start | bytes 3145732
  1203.9 3.0 copy-start.51
  1203.9 3.1 copy-start.75
  1837.1 4.9 copy-start.61
  1842.0 3.7 copy-start.60
  1845.7 3.7 copy-start.59
  1849.5 3.7 copy-start.58
  1853.2 3.1 copy-start.1
  (44 other events, 74.2 us)
Sparse Core Ops, SparseCore 0:
  37.9 118.8 all-gather.11
  175.3 98.6 all-gather.7
  275.5 34.4 all-gather.9
  330.8 71.6 reduce-scatter.13
  405.6 44.5 reduce-scatter.11
  466.6 114.8 all-gather.13
  643.7 354.3 all-reduce.7
  1001.9 64.8 reduce-scatter.19
  1070.2 63.7 reduce-scatter.17
  1138.2 63.8 reduce-scatter.15
  1207.3 629.7 all-reduce.5
